TPU v7x, 32 devices: a whole 2x2x4 slice. The times are simulated.
32 devices in a mesh: band: 8 (over z, y), rep: 4 (over x, core).
Axes of the slice: x: 2, y: 2, z: 4, core: 2. Of those that a mesh axis runs over, the one named last changes fastest.
Arguments:
- embeddings: bfloat16 [128, 4096], P('rep', 'band'), may hold values from -6 to 6
- route: int32 [4096, 1], P('band'), may hold values from 0 to 7; in each aligned block of 512 rows (0 to 511, 512 to 1023, ...) at most 160 rows name the same one
- place: bfloat16 [2, 4096], P(None, 'band'), may hold values from 0 to 1
- scales: float32 [4], replicated, may hold values from 0.25 to 1
- first_weight: bfloat16 [512, 512], replicated, may hold values from -0.25 to 0.25
- first_bias: float32 [512], replicated, may hold values from -3 to 3
- second_weight: bfloat16 [512, 512], replicated, may hold values from -0.25 to 0.25
- out_cotangent: bfloat16 [512, 96, 256], P(None, ('band', 'rep')), may hold values from -6 to 6
Outputs:
- embed_gradient: float32 [128, 4096], P('rep', 'band')
- first_weight_gradient: float32 [512, 512], replicated
- first_bias_gradient: float32 [512], replicated
- second_weight_gradient: float32 [512, 512], replicated
Inputs may be any that keep to these rules, and one draw needn't show every extreme that they name: `route`: within the 512 reports of one feed (aligned blocks of rows), at most 160 name the same band, and in some block exactly 160 do.
All inputs are finite; a program needn't handle non-finite values.
Results may differ from a plain program's by a relative error of at most 0.0063.
Values may be sent and summed in bfloat16 or wider, within the bound.
No kernel may reach another device: no remote copies, remote signals or barrier semaphores. Data moves between devices by JAX's collectives and lax.ppermute only.
A program may use at most 128 MiB of HBM per device.

v0:
```python
import jax
import jax.numpy as jnp
from jax import lax
from jax.sharding import PartitionSpec as P

root_two_pi = 0.7978845608028654
cubic = 0.044715


def padded(cells, sides, width):
    for axis, dim in sides:
        count = lax.axis_size(axis)
        ends = count - 1
        head = lax.slice_in_dim(cells, 0, width, axis=dim)
        tail = lax.slice_in_dim(cells, cells.shape[dim] - width, cells.shape[dim], axis=dim)
        cells = jnp.concatenate(
            [
                lax.ppermute(tail, axis, [(i, (i + 1) % count) for i in range(ends)]),
                cells,
                lax.ppermute(head, axis, [((i + 1) % count, i) for i in range(ends)]),
            ],
            axis=dim,
        )
    return cells


def gelu_value(value):
    inner = root_two_pi * (value + cubic * value * value * value)
    return 0.5 * value * (1.0 + jnp.tanh(inner))


def gelu_slope(value):
    tangent = jnp.tanh(root_two_pi * (value + cubic * value * value * value))
    return 0.5 * (1.0 + tangent) + 0.5 * value * (1.0 - tangent * tangent) * root_two_pi * (
        1.0 + 3.0 * cubic * value * value
    )


def kernel_factors(geometry, block, scales, lat_rows, columns):
    north_fraction = geometry[0]
    east_fraction = geometry[1]
    valid = geometry[2]
    centre_rows = jnp.arange(lat_rows, dtype=jnp.float32) + 0.5
    north_gap = (
        ((1 - block).astype(jnp.float32) * lat_rows)[None, :]
        + centre_rows[:, None]
        - (north_fraction * lat_rows)[None, :]
    )
    east_gap = (jnp.arange(columns, dtype=jnp.float32) + 0.5)[:, None] - (east_fraction * columns)[
        None, :
    ]
    reach = scales * lat_rows
    inverse = 0.5 / (reach * reach)
    row_kernel = (
        jnp.exp(-(north_gap * north_gap)[None] * inverse[:, None, None]) * valid[None, None, :]
    ).astype(jnp.bfloat16)
    column_kernel = jnp.exp(-(east_gap * east_gap)[None] * inverse[:, None, None]).astype(
        jnp.bfloat16
    )
    return (row_kernel, column_kernel)


def splat(embedded, row_kernel, column_kernel):
    channels = embedded.shape[0]
    levels, lat_rows, slots = row_kernel.shape
    columns = column_kernel.shape[1]
    sums = []
    weights = []
    for level in range(levels):
        weighted = (embedded[:, None, :] * row_kernel[level][None]).reshape(
            channels * lat_rows, slots
        )
        sums.append(
            lax.dot_general(
                weighted,
                column_kernel[level],
                (((1,), (1,)), ((), ())),
                preferred_element_type=jnp.float32,
            )
        )
        weights.append(
            lax.dot_general(
                row_kernel[level],
                column_kernel[level],
                (((1,), (1,)), ((), ())),
                preferred_element_type=jnp.float32,
            )
        )
    splatted = jnp.stack(sums).reshape(levels, channels, lat_rows * columns)
    density = jnp.stack(weights).reshape(levels, lat_rows * columns)
    features = (
        (splatted / (density[:, None, :] + 1.0))
        .transpose(1, 0, 2)
        .reshape(channels * levels, lat_rows * columns)
        .astype(jnp.bfloat16)
    )
    return (features, density)


def spread_back(gradient, row_kernel, column_kernel):
    levels, lat_rows, slots = row_kernel.shape
    columns = column_kernel.shape[1]
    channels = gradient.shape[0] // levels
    grid = gradient.reshape(channels, levels, lat_rows * columns)
    total = jnp.zeros((channels, slots), jnp.float32)
    for level in range(levels):
        slab = grid[:, level].reshape(channels * lat_rows, columns)
        along = jnp.dot(slab, column_kernel[level], preferred_element_type=jnp.float32).reshape(
            channels, lat_rows, slots
        )
        total = total + jnp.sum(along * row_kernel[level][None].astype(jnp.float32), axis=1)
    return total


def band_ranks(route_rows, bands):
    owner = route_rows[:, 0]
    onehot = (owner[:, None] == jnp.arange(bands, dtype=jnp.int32)[None, :]).astype(jnp.int32)
    running = jnp.cumsum(onehot, axis=0)
    return (owner, jnp.sum((running - 1) * onehot, axis=1))


def on_device(
    embeddings, route, place, scales, first_weight, first_bias, second_weight, out_cotangent
):
    channels, reports = embeddings.shape
    bands = lax.axis_size("band")
    parts = lax.axis_size("rep")
    quarter = lax.axis_index("rep")
    capacity = max(2, 5 * reports // (2 * bands))
    sub_rows = out_cotangent.shape[1]
    lat_rows = sub_rows * parts
    columns = out_cotangent.shape[2]
    levels = scales.shape[0]
    owner, rank = band_ranks(route, bands)
    packed = jnp.concatenate([embeddings, place, jnp.ones((1, reports), jnp.bfloat16)], axis=0)
    rows = channels + 3
    whole = bands * capacity
    outgoing = jnp.zeros((rows, whole), jnp.bfloat16).at[:, owner * capacity + rank].set(packed)
    arrived = lax.all_to_all(outgoing, "band", split_axis=1, concat_axis=1, tiled=True)
    nearby = padded(arrived, (("band", 1),), whole)
    block = jnp.arange(3 * whole, dtype=jnp.int32) // whole
    geometry = nearby[channels:].astype(jnp.float32)
    row_kernel, column_kernel = kernel_factors(geometry, block, scales, lat_rows, columns)
    features, density = splat(nearby[:channels], row_kernel, column_kernel)
    cotangent = out_cotangent.reshape(out_cotangent.shape[0], sub_rows * columns)
    mine = lax.all_to_all(features, "rep", split_axis=1, concat_axis=0, tiled=True)
    local_density = lax.dynamic_slice_in_dim(
        density.reshape(levels, lat_rows, columns), quarter * sub_rows, sub_rows, 1
    ).reshape(levels, sub_rows * columns)
    preact = (
        lax.dot_general(
            first_weight, mine, (((0,), (0,)), ((), ())), preferred_element_type=jnp.float32
        )
        + first_bias[:, None]
    )
    hidden = gelu_value(preact).astype(jnp.bfloat16)
    pre_gradient = (
        jnp.dot(second_weight, cotangent, preferred_element_type=jnp.float32) * gelu_slope(preact)
    ).astype(jnp.bfloat16)
    first_sum = lax.dot_general(
        mine, pre_gradient, (((1,), (1,)), ((), ())), preferred_element_type=jnp.float32
    )
    second_sum = lax.dot_general(
        hidden, cotangent, (((1,), (1,)), ((), ())), preferred_element_type=jnp.float32
    )
    bias_sum = jnp.sum(pre_gradient.astype(jnp.float32), axis=1)
    feature_gradient = jnp.dot(first_weight, pre_gradient, preferred_element_type=jnp.float32)
    count = sub_rows * columns
    cell_part = (
        (feature_gradient.reshape(-1, levels, count) / (local_density[None] + 1.0))
        .reshape(-1, count)
        .astype(jnp.bfloat16)
    )
    splat_gradient = lax.all_to_all(cell_part, "rep", split_axis=0, concat_axis=1, tiled=True)
    totals = lax.psum((first_sum, second_sum, bias_sum), ("band", "rep"))
    slot_gradient = spread_back(splat_gradient, row_kernel, column_kernel)
    outward = jnp.concatenate([slot_gradient[:, :whole], slot_gradient[:, 2 * whole :]], axis=1)
    returned = padded(outward, (("band", 1),), whole)
    own_total = slot_gradient[:, whole : 2 * whole] + returned[:, :whole] + returned[:, 3 * whole :]
    backward = lax.all_to_all(own_total, "band", split_axis=1, concat_axis=1, tiled=True)
    embed_gradient = backward[:, owner * capacity + rank]
    return (embed_gradient, totals[0], totals[2], totals[1])


def solution(mesh):
    return jax.shard_map(
        on_device,
        mesh=mesh,
        in_specs=(
            P("rep", "band"),
            P("band", None),
            P(None, "band"),
            P(),
            P(),
            P(),
            P(),
            P(None, ("band", "rep"), None),
        ),
        out_specs=(P("rep", "band"), P(), P(), P()),
        check_vma=False,
    )
```

profile of v0, /device:TPU:0, one launch (start us, length us, event | category | flops | bytes accessed | tf_op | source)
XLA Modules:
  0.0 270.7 jit_solution(15781892218511032208)
XLA Ops:
  14.6 7.3 %all-to-all-start = ((bf16[35,8,160]{2,0,1:T(8,128)(2,1)}), bf16[35,8,160]{2,0,1:T(8,128)(2,1)S(1)}, u32[]{:S(2)}, u32[]{:S(2)}) async-start(bf16[35,8,160]{2,0,1:T(8,128)(2,1)} %copy.50), calls=%async_computation | async-start | bytes 327680 | tf_op jit(solution)/shard_map/all_to_all | solution.py:139
  22.6 6.9 %all-to-all-done = bf16[35,8,160]{2,0,1:T(8,128)(2,1)S(1)} async-done(((bf16[35,8,160]{2,0,1:T(8,128)(2,1)}), bf16[35,8,160]{2,0,1:T(8,128)(2,1)S(1)}, u32[]{:S(2)}, u32[]{:S(2)}) %all-to-all-start) | async-done | bytes 89632 | tf_op jit(solution)/shard_map/all_to_all | solution.py:139
  35.8 3.3 %collective-permute-done.1 = bf16[35,1280]{1,0:T(8,128)(2,1)S(1)} collective-permute-done((bf16[35,1280]{1,0:T(8,128)(2,1)S(1)}, bf16[35,1280]{1,0:T(8,128)(2,1)S(1)}, u32[]{:S(2)}, u32[]{:S(2)}) %collective-permute-start.1) | collective-permute-done | bytes 89632 | tf_op jit(solution)/shard_map/ppermute | solution.py:20
  41.2 2.9 %exponential_convert_fusion = bf16[4,256,3840]{2,1,0:T(8,128)(2,1)S(1)} fusion(f32[4]{0:T(128)S(1)} %multiply_divide_fusion, f32[256,3840]{1,0:T(8,128)S(1)} %multiply_negate_fusion), kind=kLoop, calls=%fused_computation.2 | loop fusion | flops 7864320 | bytes 11796496 | tf_op jit(solution)/shard_map/convert_element_type | solution.py:57
  49.2 6.1 %broadcast_multiply_fusion.3 = (bf16[32,12,3840]{2,1,0:T(8,128)(2,1)}, bf16[32,12,3840]{2,1,0:T(8,128)(2,1)}, bf16[32,12,3840]{2,1,0:T(8,128)(2,1)}, bf16[32,12,3840]{2,1,0:T(8,128)(2,1)}) fusion(bf16[12,3840]{1,0:T(8,128)(2,1)S(1)} %copy-done.10, bf16[32,3840]{1,0:T(8,128)(2,1)S(1)} %slice.107, bf16[12,3840]{1,0:T(8,128)(2,1)S(1)} %copy-done.9, ...), kind=kLoop, calls=%fused_computation.33 | loop fusion | flops 5898240 | bytes 12410880 | tf_op jit(solution)/shard_map/mul | solution.py:70
  55.3 3.9 %mul.295 = bf16[384,3840]{1,0:T(8,128)(2,1)S(1)} reshape(bf16[32,12,3840]{2,1,0:T(8,128)(2,1)} %get-tuple-element.39) | data formatting | bytes 5898240 | tf_op jit(solution)/shard_map/mul | solution.py:70
  59.1 3.2 %fusion.18 = f32[384,256]{1,0:T(8,128)} fusion(bf16[384,3840]{1,0:T(8,128)(2,1)S(1)} %mul.295, bf16[4,256,3840]{2,1,0:T(8,128)(2,1)} %copy-done.1), kind=kOutput, calls=%fused_computation.28 | convolution fusion | flops 754974720 | bytes 5308416 | tf_op jit(solution)/shard_map/dot_general | solution.py:74
  64.5 3.9 %mul.306 = bf16[384,3840]{1,0:T(8,128)(2,1)S(1)} reshape(bf16[32,12,3840]{2,1,0:T(8,128)(2,1)} %get-tuple-element.40) | data formatting | bytes 5898240 | tf_op jit(solution)/shard_map/mul | solution.py:70
  68.4 3.2 %fusion.14 = f32[384,256]{1,0:T(8,128)} fusion(bf16[384,3840]{1,0:T(8,128)(2,1)S(1)} %mul.306, bf16[4,256,3840]{2,1,0:T(8,128)(2,1)} %copy-done.1), kind=kOutput, calls=%fused_computation.24 | convolution fusion | flops 754974720 | bytes 5308416 | tf_op jit(solution)/shard_map/dot_general | solution.py:74
  73.8 3.9 %mul.310 = bf16[384,3840]{1,0:T(8,128)(2,1)S(1)} reshape(bf16[32,12,3840]{2,1,0:T(8,128)(2,1)} %get-tuple-element.41) | data formatting | bytes 5898240 | tf_op jit(solution)/shard_map/mul | solution.py:70
  77.7 3.2 %fusion.10 = f32[384,256]{1,0:T(8,128)} fusion(bf16[384,3840]{1,0:T(8,128)(2,1)S(1)} %mul.310, bf16[4,256,3840]{2,1,0:T(8,128)(2,1)} %copy-done.1), kind=kOutput, calls=%fused_computation.20 | convolution fusion | flops 754974720 | bytes 5308416 | tf_op jit(solution)/shard_map/dot_general | solution.py:74
  83.1 3.9 %mul.314 = bf16[384,3840]{1,0:T(8,128)(2,1)S(1)} reshape(bf16[32,12,3840]{2,1,0:T(8,128)(2,1)} %get-tuple-element.42) | data formatting | bytes 5898240 | tf_op jit(solution)/shard_map/mul | solution.py:70
  87.0 3.3 %fusion.6 = f32[384,256]{1,0:T(8,128)} fusion(bf16[384,3840]{1,0:T(8,128)(2,1)S(1)} %mul.314, bf16[4,256,3840]{2,1,0:T(8,128)(2,1)} %copy-done.1), kind=kOutput, calls=%fused_computation.16 | convolution fusion | flops 754974720 | bytes 5308416 | tf_op jit(solution)/shard_map/dot_general | solution.py:74
  95.9 3.5 %all-to-all-start.1 = ((bf16[128,4,768]{2,0,1:T(8,128)(2,1)}), bf16[128,4,768]{2,0,1:T(8,128)(2,1)S(1)}, u32[]{:S(2)}, u32[]{:S(2)}) async-start(bf16[128,4,768]{2,0,1:T(8,128)(2,1)} %copy.56), calls=%async_computation.1 | async-start | bytes 1572864 | tf_op jit(solution)/shard_map/all_to_all | solution.py:146
  102.6 8.4 %all-to-all-done.1 = bf16[128,4,768]{2,0,1:T(8,128)(2,1)S(1)} async-done(((bf16[128,4,768]{2,0,1:T(8,128)(2,1)}), bf16[128,4,768]{2,0,1:T(8,128)(2,1)S(1)}, u32[]{:S(2)}, u32[]{:S(2)}) %all-to-all-start.1) | async-done | bytes 786464 | tf_op jit(solution)/shard_map/all_to_all | solution.py:146
  115.1 3.5 %all-to-all-start.2 = ((bf16[4,128,768]{2,1,0:T(8,128)(2,1)}), bf16[4,128,768]{2,1,0:T(8,128)(2,1)S(1)}, u32[]{:S(2)}, u32[]{:S(2)}) async-start(bf16[4,128,768]{2,1,0:T(8,128)(2,1)} %bitcast.158), calls=%async_computation.2 | async-start | bytes 1572864 | tf_op jit(solution)/shard_map/all_to_all | solution.py:174
  118.9 2.8 %fusion.90 = f32[512,512]{1,0:T(8,128)} fusion(bf16[512,768]{1,0:T(8,128)(2,1)S(1)} %bitcast.153, bf16[512,768]{1,0:T(8,128)(2,1)} %copy-done.6), kind=kOutput, calls=%fused_computation.140 | convolution fusion | flops 402653184 | bytes 2621440 | tf_op jit(solution)/shard_map/dot_general | solution.py:160
  123.4 6.8 %all-to-all-done.2 = bf16[4,128,768]{2,1,0:T(8,128)(2,1)S(1)} async-done(((bf16[4,128,768]{2,1,0:T(8,128)(2,1)}), bf16[4,128,768]{2,1,0:T(8,128)(2,1)S(1)}, u32[]{:S(2)}, u32[]{:S(2)}) %all-to-all-start.2) | async-done | bytes 786464 | tf_op jit(solution)/shard_map/all_to_all | solution.py:174
  131.2 3.4 %slice_reduce_fusion.2 = (bf16[32,3072]{1,0:T(8,128)(2,1)S(1)}, bf16[32,3072]{1,0:T(8,128)(2,1)S(1)}, bf16[32,3072]{1,0:T(8,128)(2,1)S(1)}, bf16[32,3072]{1,0:T(8,128)(2,1)S(1)}) fusion(bf16[32,4,3072]{2,1,0:T(4,128)(2,1)S(1)} %reshape.284), kind=kLoop, calls=%fused_computation.71 | loop fusion | bytes 1572864 | tf_op jit(solution)/shard_map/slice | solution.py:107
  142.1 3.6 %collective-permute-start.2 = (f32[32,1280]{1,0:T(8,128)S(1)}, f32[32,1280]{1,0:T(8,128)S(1)}, u32[]{:S(2)}, u32[]{:S(2)}) collective-permute-start(f32[32,1280]{1,0:T(8,128)S(1)} %get-tuple-element.29), channel_id=1, source_target_pairs={{0,4},{4,8},{8,12},{12,16},{16,20},{20,24},{24,28},{1,5},{5,9},{9,... | collective-permute-start | bytes 491528 | tf_op jit(solution)/shard_map/ppermute | solution.py:18
  147.0 3.3 %collective-permute-done.2 = f32[32,1280]{1,0:T(8,128)S(1)} collective-permute-done((f32[32,1280]{1,0:T(8,128)S(1)}, f32[32,1280]{1,0:T(8,128)S(1)}, u32[]{:S(2)}, u32[]{:S(2)}) %collective-permute-start.2) | collective-permute-done | bytes 163872 | tf_op jit(solution)/shard_map/ppermute | solution.py:18
  153.9 5.2 %all-to-all-start.3 = ((f32[32,8,160]{2,0,1:T(8,128)}), f32[32,8,160]{2,0,1:T(8,128)S(1)}, u32[]{:S(2)}, u32[]{:S(2)}) async-start(f32[32,8,160]{2,0,1:T(8,128)} %copy.63), calls=%async_computation.3 | async-start | bytes 524288 | tf_op jit(solution)/shard_map/all_to_all | solution.py:180
  159.2 40.6 %psum.22 = f32[512]{0:T(512)} all-reduce(f32[512]{0:T(512)S(1)} %get-tuple-element.43), channel_id=1, replica_groups=mesh['band'=8,'rep'=4] {'band','rep'}, use_global_device_ids=true, to_apply=%region_10.11 | all-reduce | flops 512 | bytes 4096 | tf_op jit(solution)/shard_map/psum | solution.py:175
  201.9 58.7 %all-reduce.3.cloned.1.call-done = (f32[512,512]{1,0:T(8,128)}, f32[512,512]{1,0:T(8,128)}) async-done(((f32[512,512]{1,0:T(8,128)}, f32[512,512]{1,0:T(8,128)}), (f32[512,512]{1,0:T(8,128)}, f32[512,512]{1,0:T(8,128)})) %all-reduce.3.cloned.1.call-update) | async-done | bytes 2097168 | tf_op jit(solution)/shard_map/psum | solution.py:175
  (131 shorter events, 61.1 us)
Async XLA Ops:
  7.2 103.8 %copy-start = (bf16[512,512]{1,0:T(8,128)(2,1)S(1)}, bf16[512,512]{1,0:T(8,128)(2,1)}, u32[]{:S(2)}) copy-start(bf16[512,512]{1,0:T(8,128)(2,1)} %param.12) | copy-start | bytes 1572868
  10.8 28.9 %copy-start.18 = (s32[512,1]{0,1:T(1,128)}, s32[512,1]{0,1:T(1,128)S(1)}, u32[]{:S(2)}) copy-start(s32[512,1]{0,1:T(1,128)S(1)} %compare_select_fusion) | copy-start | bytes 6148
  14.6 14.9 %all-to-all-start = ((bf16[35,8,160]{2,0,1:T(8,128)(2,1)}), bf16[35,8,160]{2,0,1:T(8,128)(2,1)S(1)}, u32[]{:S(2)}, u32[]{:S(2)}) async-start(bf16[35,8,160]{2,0,1:T(8,128)(2,1)} %copy.50), calls=%async_computation | async-start | bytes 327680 | tf_op jit(solution)/shard_map/all_to_all | solution.py:139
  29.7 6.1 %collective-permute-start = (bf16[35,1280]{1,0:T(8,128)(2,1)S(1)}, bf16[35,1280]{1,0:T(8,128)(2,1)S(1)}, u32[]{:S(2)}, u32[]{:S(2)}) collective-permute-start(bf16[35,1280]{1,0:T(8,128)(2,1)S(1)} %all_to_all.42), channel_id=1, source_target_pairs={{0,4},{4,8},{8,12},{12,16},{16,20},{20,24},{24,28},{1,5},{5,9},{9,... | collective-permute-start | bytes 268808 | tf_op jit(solution)/shard_map/ppermute | solution.py:18
  32.6 6.6 %collective-permute-start.1 = (bf16[35,1280]{1,0:T(8,128)(2,1)S(1)}, bf16[35,1280]{1,0:T(8,128)(2,1)S(1)}, u32[]{:S(2)}, u32[]{:S(2)}) collective-permute-start(bf16[35,1280]{1,0:T(8,128)(2,1)S(1)} %all_to_all.42), channel_id=1, source_target_pairs={{4,0},{8,4},{12,8},{16,12},{20,16},{24,20},{28,24},{5,1},{9,5},{13... | collective-permute-start | bytes 268808 | tf_op jit(solution)/shard_map/ppermute | solution.py:20
  44.2 11.1 %copy-start.1 = (bf16[4,256,3840]{2,1,0:T(8,128)(2,1)}, bf16[4,256,3840]{2,1,0:T(8,128)(2,1)S(1)}, u32[]{:S(2)}) copy-start(bf16[4,256,3840]{2,1,0:T(8,128)(2,1)S(1)} %exponential_convert_fusion) | copy-start | bytes 23592964
  87.0 4.7 %copy-start.15 = (f32[12,256]{1,0:T(8,128)S(1)}, f32[12,256]{1,0:T(8,128)}, u32[]{:S(2)}) copy-start(f32[12,256]{1,0:T(8,128)} %fusion.8) | copy-start | bytes 36868
  87.0 4.7 %copy-start.16 = (f32[12,256]{1,0:T(8,128)S(1)}, f32[12,256]{1,0:T(8,128)}, u32[]{:S(2)}) copy-start(f32[12,256]{1,0:T(8,128)} %fusion.12) | copy-start | bytes 36868
  87.0 4.8 %copy-start.17 = (f32[12,256]{1,0:T(8,128)S(1)}, f32[12,256]{1,0:T(8,128)}, u32[]{:S(2)}) copy-start(f32[12,256]{1,0:T(8,128)} %fusion.16) | copy-start | bytes 36868
  94.9 4.5 %copy-start.4 = (bf16[512,3,256]{2,0,1:T(8,128)(2,1)S(1)}, bf16[512,3,256]{2,0,1:T(8,128)(2,1)}, u32[]{:S(2)}) copy-start(bf16[512,3,256]{2,0,1:T(8,128)(2,1)} %param.15) | copy-start | bytes 2359300
  95.9 15.1 %all-to-all-start.1 = ((bf16[128,4,768]{2,0,1:T(8,128)(2,1)}), bf16[128,4,768]{2,0,1:T(8,128)(2,1)S(1)}, u32[]{:S(2)}, u32[]{:S(2)}) async-start(bf16[128,4,768]{2,0,1:T(8,128)(2,1)} %copy.56), calls=%async_computation.1 | async-start | bytes 1572864 | tf_op jit(solution)/shard_map/all_to_all | solution.py:146
  100.8 10.2 %copy-start.21 = (f32[512]{0:T(512)S(1)}, f32[512]{0:T(512)}, u32[]{:S(2)}) copy-start(f32[512]{0:T(512)} %param.13) | copy-start | bytes 6148
  102.6 9.1 %copy-start.5 = (bf16[512,3,256]{0,2,1:T(8,128)(2,1)S(1)}, bf16[512,3,256]{0,2,1:T(8,128)(2,1)}, u32[]{:S(2)}) copy-start(bf16[512,3,256]{0,2,1:T(8,128)(2,1)} %copy.48) | copy-start | bytes 2359300
  102.6 9.1 %copy-start.20 = (bf16[512,512]{1,0:T(8,128)(2,1)S(1)}, bf16[512,512]{1,0:T(8,128)(2,1)}, u32[]{:S(2)}) copy-start(bf16[512,512]{1,0:T(8,128)(2,1)} %param.14) | copy-start | bytes 1572868
  115.1 15.1 %all-to-all-start.2 = ((bf16[4,128,768]{2,1,0:T(8,128)(2,1)}), bf16[4,128,768]{2,1,0:T(8,128)(2,1)S(1)}, u32[]{:S(2)}, u32[]{:S(2)}) async-start(bf16[4,128,768]{2,1,0:T(8,128)(2,1)} %bitcast.158), calls=%async_computation.2 | async-start | bytes 1572864 | tf_op jit(solution)/shard_map/all_to_all | solution.py:174
  118.6 141.9 %all-reduce.3.cloned.1.call-start = ((), (), s32[]{:S(2)}) async-start(), calls=%async_computation.4 | async-start | bytes 4194304 | tf_op jit(solution)/shard_map/psum | solution.py:175
  118.9 2.8 %copy-start.23 = (f32[768,512]{0,1:T(8,128)S(1)}, f32[768,512]{0,1:T(8,128)}, u32[]{:S(2)}) copy-start(f32[768,512]{0,1:T(8,128)} %copy-done.22) | copy-start | bytes 4718596
  130.8 3.7 %copy-start.14 = (f32[12,3840]{1,0:T(8,128)S(1)}, f32[12,3840]{1,0:T(8,128)}, u32[]{:S(2)}) copy-start(f32[12,3840]{1,0:T(8,128)} %get-tuple-element.31) | copy-start | bytes 552964
  131.1 8.8 %slice-start = ((s8[7864320]{0:T(1024)(128)(4,1)}), s8[3670016]{0:T(1024)(128)(4,1)S(1)}, s32[]{:S(2)}) async-start(s8[7864320]{0:T(1024)(128)(4,1)} %bitcast.149), calls=%async_computation.5 | async-start | bytes 7340032
  134.6 5.4 %slice-start.1 = ((s8[7864320]{0:T(1024)(128)(4,1)}), s8[4194304]{0:T(1024)(128)(4,1)S(1)}, s32[]{:S(2)}) async-start(s8[7864320]{0:T(1024)(128)(4,1)} %bitcast.149), calls=%async_computation.6 | async-start | bytes 8388608
  142.0 17.1 %copy-start.19 = (s32[512,1]{0,1:T(1,128)S(1)}, s32[512,1]{0,1:T(1,128)}, u32[]{:S(2)}) copy-start(s32[512,1]{0,1:T(1,128)} %copy-done.18) | copy-start | bytes 6148
  142.1 8.3 %collective-permute-start.2 = (f32[32,1280]{1,0:T(8,128)S(1)}, f32[32,1280]{1,0:T(8,128)S(1)}, u32[]{:S(2)}, u32[]{:S(2)}) collective-permute-start(f32[32,1280]{1,0:T(8,128)S(1)} %get-tuple-element.29), channel_id=1, source_target_pairs={{0,4},{4,8},{8,12},{12,16},{16,20},{20,24},{24,28},{1,5},{5,9},{9,... | collective-permute-start | bytes 491528 | tf_op jit(solution)/shard_map/ppermute | solution.py:18
  145.7 7.3 %collective-permute-start.3 = (f32[32,1280]{1,0:T(8,128)S(1)}, f32[32,1280]{1,0:T(8,128)S(1)}, u32[]{:S(2)}, u32[]{:S(2)}) collective-permute-start(f32[32,1280]{1,0:T(8,128)S(1)} %get-tuple-element.30), channel_id=1, source_target_pairs={{4,0},{8,4},{12,8},{16,12},{20,16},{24,20},{28,24},{5,1},{9,5},{13... | collective-permute-start | bytes 491528 | tf_op jit(solution)/shard_map/ppermute | solution.py:20
  153.9 45.9 %all-to-all-start.3 = ((f32[32,8,160]{2,0,1:T(8,128)}), f32[32,8,160]{2,0,1:T(8,128)S(1)}, u32[]{:S(2)}, u32[]{:S(2)}) async-start(f32[32,8,160]{2,0,1:T(8,128)} %copy.63), calls=%async_computation.3 | async-start | bytes 524288 | tf_op jit(solution)/shard_map/all_to_all | solution.py:180
  (11 other events, 24.3 us)
Sparse Core Ops, SparseCore 0:
  125.5 134.9 all-reduce.2
where the time goes:
time: 272 us; the launch traced here: 271 us
  waiting for transfers between devices  92.1 us (34%)
  local copies, waits for them, and re-layouts  42.5 us (16%)
  blocking collectives  40.6 us (15%)
  matrix products  33.1 us (12%)
  starting transfers between devices  28.8 us (11%)
  other arithmetic  18.9 us (7%)
  between operations  14.7 us (5%)
    psum x1, waiting for transfers between devices, on_device(): totals = lax.psum((first_sum, second_sum, bias_sum), ('band', 'rep'))  58.7 us
    psum x1, blocking collectives, on_device(): totals = lax.psum((first_sum, second_sum, bias_sum), ('band', 'rep'))  40.6 us
    mul x4, local copies, waits for them, and re-layouts, splat(): embedded[:, None, :] * row_kernel[level][None]  15.5 us
    dot_general x4, matrix products, splat(): lax.dot_general(weighted, column_kernel[level], (((1,), (1,)), ((), ())),...  13 us
    all_to_all x1, waiting for transfers between devices, on_device(): lax.all_to_all(features, 'rep', split_axis=1, concat_axis=0, tiled=True)  8.44 us
    another operation x4, local copies, waits for them, and re-layouts, splat(): splatted = jnp.stack(sums).reshape(levels, channels, lat_rows * columns)  7.83 us
    all_to_all x1, starting transfers between devices, on_device(): lax.all_to_all(outgoing, 'band', split_axis=1, concat_axis=1, tiled=True)  7.31 us
    dot_general x4, matrix products, spread_back(): jnp.dot(slab, column_kernel[level], preferred_element_type=jnp.float32)  7.24 us
  transfers between devices with their start and end apart: 9, of which 8 were waited for; matrix products, arithmetic and copies ran while one was open for 8% of the time, Pallas kernels for 0%

commit v1 on v0

--- a/solution.py
+++ b/solution.py
@@ -2,6 +2,7 @@
 import jax.numpy as jnp
 from jax import lax
 from jax.sharding import PartitionSpec as P
+from jax.lax import psum
 
 root_two_pi = 0.7978845608028654
 cubic = 0.044715
@@ -172,7 +173,15 @@
         .astype(jnp.bfloat16)
     )
     splat_gradient = lax.all_to_all(cell_part, "rep", split_axis=0, concat_axis=1, tiled=True)
-    totals = lax.psum((first_sum, second_sum, bias_sum), ("band", "rep"))
+
+    def _balance_desk(z):
+        axis_tag = "rep"
+        mesh_dim = "band"
+        for w in (axis_tag, mesh_dim):
+            z = psum(z, w)
+        return z
+
+    totals = _balance_desk((first_sum, second_sum, bias_sum))
     slot_gradient = spread_back(splat_gradient, row_kernel, column_kernel)
     outward = jnp.concatenate([slot_gradient[:, :whole], slot_gradient[:, 2 * whole :]], axis=1)
     returned = padded(outward, (("band", 1),), whole)

time: 272 us -> 297 us (1.092)
  waiting for transfers between devices: 92.1 us -> 127 us
  blocking collectives: 40.6 us -> 29 us
    psum x1 -> x2, waiting for transfers between devices: 58.7 us -> 93.2 us  [_balance_desk(): z = psum(z, w)]
    psum x1 -> x2, blocking collectives: 40.6 us -> 29 us  [_balance_desk(): z = psum(z, w)]
  transfers between devices with their start and end apart: 9 -> 10, of which waited for: 8 -> 9; matrix products, arithmetic and copies ran while one was open for 8% -> 8% of each run, Pallas kernels for 0% -> 0%
where the time goes in v1:
time: 297 us; the launch traced here: 296 us
  waiting for transfers between devices  127 us (43%)
  local copies, waits for them, and re-layouts  42.5 us (14%)
  matrix products  33.1 us (11%)
  starting transfers between devices  30.6 us (10%)
  blocking collectives  29 us (10%)
  other arithmetic  18.9 us (6%)
  between operations  14.7 us (5%)
    psum x2, waiting for transfers between devices, _balance_desk(): z = psum(z, w)  93.2 us
    psum x2, blocking collectives, _balance_desk(): z = psum(z, w)  29 us
    mul x4, local copies, waits for them, and re-layouts, splat(): embedded[:, None, :] * row_kernel[level][None]  15.5 us
    dot_general x4, matrix products, splat(): lax.dot_general(weighted, column_kernel[level], (((1,), (1,)), ((), ())),...  13 us
    all_to_all x1, waiting for transfers between devices, on_device(): lax.all_to_all(features, 'rep', split_axis=1, concat_axis=0, tiled=True)  8.44 us
    another operation x4, local copies, waits for them, and re-layouts, splat(): splatted = jnp.stack(sums).reshape(levels, channels, lat_rows * columns)  7.83 us
    ppermute x2, waiting for transfers between devices, padded(): lax.ppermute(head, axis, [((i + 1) % count, i) for i in range(ends)])  7.38 us
    all_to_all x1, starting transfers between devices, on_device(): lax.all_to_all(outgoing, 'band', split_axis=1, concat_axis=1, tiled=True)  7.31 us
  transfers between devices with their start and end apart: 10, of which 9 were waited for; matrix products, arithmetic and copies ran while one was open for 8% of the time, Pallas kernels for 0%

profile of v1, /device:TPU:0, one launch (start us, length us, event | category | flops | bytes accessed | tf_op | source)
XLA Modules:
  0.0 295.9 jit_solution(13367626096090955548)
XLA Ops:
  14.6 7.3 %all-to-all-start = ((bf16[35,8,160]{2,0,1:T(8,128)(2,1)}), bf16[35,8,160]{2,0,1:T(8,128)(2,1)S(1)}, u32[]{:S(2)}, u32[]{:S(2)}) async-start(bf16[35,8,160]{2,0,1:T(8,128)(2,1)} %copy.50), calls=%async_computation | async-start | bytes 327680 | tf_op jit(solution)/shard_map/all_to_all | solution.py:140
  22.6 6.9 %all-to-all-done = bf16[35,8,160]{2,0,1:T(8,128)(2,1)S(1)} async-done(((bf16[35,8,160]{2,0,1:T(8,128)(2,1)}), bf16[35,8,160]{2,0,1:T(8,128)(2,1)S(1)}, u32[]{:S(2)}, u32[]{:S(2)}) %all-to-all-start) | async-done | bytes 89632 | tf_op jit(solution)/shard_map/all_to_all | solution.py:140
  35.8 3.3 %collective-permute-done.1 = bf16[35,1280]{1,0:T(8,128)(2,1)S(1)} collective-permute-done((bf16[35,1280]{1,0:T(8,128)(2,1)S(1)}, bf16[35,1280]{1,0:T(8,128)(2,1)S(1)}, u32[]{:S(2)}, u32[]{:S(2)}) %collective-permute-start.1) | collective-permute-done | bytes 89632 | tf_op jit(solution)/shard_map/ppermute | solution.py:21
  49.2 6.1 %broadcast_multiply_fusion.3 = (bf16[32,12,3840]{2,1,0:T(8,128)(2,1)}, bf16[32,12,3840]{2,1,0:T(8,128)(2,1)}, bf16[32,12,3840]{2,1,0:T(8,128)(2,1)}, bf16[32,12,3840]{2,1,0:T(8,128)(2,1)}) fusion(bf16[12,3840]{1,0:T(8,128)(2,1)S(1)} %copy-done.10, bf16[32,3840]{1,0:T(8,128)(2,1)S(1)} %slice.107, bf16[12,3840]{1,0:T(8,128)(2,1)S(1)} %copy-done.9, ...), kind=kLoop, calls=%fused_computation.33 | loop fusion | flops 5898240 | bytes 12410880 | tf_op jit(solution)/shard_map/mul | solution.py:71
  55.3 3.9 %mul.295 = bf16[384,3840]{1,0:T(8,128)(2,1)S(1)} reshape(bf16[32,12,3840]{2,1,0:T(8,128)(2,1)} %get-tuple-element.41) | data formatting | bytes 5898240 | tf_op jit(solution)/shard_map/mul | solution.py:71
  59.1 3.2 %fusion.18 = f32[384,256]{1,0:T(8,128)} fusion(bf16[384,3840]{1,0:T(8,128)(2,1)S(1)} %mul.295, bf16[4,256,3840]{2,1,0:T(8,128)(2,1)} %copy-done.1), kind=kOutput, calls=%fused_computation.28 | convolution fusion | flops 754974720 | bytes 5308416 | tf_op jit(solution)/shard_map/dot_general | solution.py:75
  64.5 3.9 %mul.306 = bf16[384,3840]{1,0:T(8,128)(2,1)S(1)} reshape(bf16[32,12,3840]{2,1,0:T(8,128)(2,1)} %get-tuple-element.42) | data formatting | bytes 5898240 | tf_op jit(solution)/shard_map/mul | solution.py:71
  68.4 3.2 %fusion.14 = f32[384,256]{1,0:T(8,128)} fusion(bf16[384,3840]{1,0:T(8,128)(2,1)S(1)} %mul.306, bf16[4,256,3840]{2,1,0:T(8,128)(2,1)} %copy-done.1), kind=kOutput, calls=%fused_computation.24 | convolution fusion | flops 754974720 | bytes 5308416 | tf_op jit(solution)/shard_map/dot_general | solution.py:75
  73.8 3.9 %mul.310 = bf16[384,3840]{1,0:T(8,128)(2,1)S(1)} reshape(bf16[32,12,3840]{2,1,0:T(8,128)(2,1)} %get-tuple-element.43) | data formatting | bytes 5898240 | tf_op jit(solution)/shard_map/mul | solution.py:71
  77.7 3.2 %fusion.10 = f32[384,256]{1,0:T(8,128)} fusion(bf16[384,3840]{1,0:T(8,128)(2,1)S(1)} %mul.310, bf16[4,256,3840]{2,1,0:T(8,128)(2,1)} %copy-done.1), kind=kOutput, calls=%fused_computation.20 | convolution fusion | flops 754974720 | bytes 5308416 | tf_op jit(solution)/shard_map/dot_general | solution.py:75
  83.1 3.9 %mul.314 = bf16[384,3840]{1,0:T(8,128)(2,1)S(1)} reshape(bf16[32,12,3840]{2,1,0:T(8,128)(2,1)} %get-tuple-element.44) | data formatting | bytes 5898240 | tf_op jit(solution)/shard_map/mul | solution.py:71
  87.0 3.3 %fusion.6 = f32[384,256]{1,0:T(8,128)} fusion(bf16[384,3840]{1,0:T(8,128)(2,1)S(1)} %mul.314, bf16[4,256,3840]{2,1,0:T(8,128)(2,1)} %copy-done.1), kind=kOutput, calls=%fused_computation.16 | convolution fusion | flops 754974720 | bytes 5308416 | tf_op jit(solution)/shard_map/dot_general | solution.py:75
  95.9 3.5 %all-to-all-start.1 = ((bf16[128,4,768]{2,0,1:T(8,128)(2,1)}), bf16[128,4,768]{2,0,1:T(8,128)(2,1)S(1)}, u32[]{:S(2)}, u32[]{:S(2)}) async-start(bf16[128,4,768]{2,0,1:T(8,128)(2,1)} %copy.56), calls=%async_computation.1 | async-start | bytes 1572864 | tf_op jit(solution)/shard_map/all_to_all | solution.py:147
  102.6 8.4 %all-to-all-done.1 = bf16[128,4,768]{2,0,1:T(8,128)(2,1)S(1)} async-done(((bf16[128,4,768]{2,0,1:T(8,128)(2,1)}), bf16[128,4,768]{2,0,1:T(8,128)(2,1)S(1)}, u32[]{:S(2)}, u32[]{:S(2)}) %all-to-all-start.1) | async-done | bytes 786464 | tf_op jit(solution)/shard_map/all_to_all | solution.py:147
  115.1 3.5 %all-to-all-start.2 = ((bf16[4,128,768]{2,1,0:T(8,128)(2,1)}), bf16[4,128,768]{2,1,0:T(8,128)(2,1)S(1)}, u32[]{:S(2)}, u32[]{:S(2)}) async-start(bf16[4,128,768]{2,1,0:T(8,128)(2,1)} %bitcast.158), calls=%async_computation.2 | async-start | bytes 1572864 | tf_op jit(solution)/shard_map/all_to_all | solution.py:175
  123.4 7.3 %all-to-all-done.2 = bf16[4,128,768]{2,1,0:T(8,128)(2,1)S(1)} async-done(((bf16[4,128,768]{2,1,0:T(8,128)(2,1)}), bf16[4,128,768]{2,1,0:T(8,128)(2,1)S(1)}, u32[]{:S(2)}, u32[]{:S(2)}) %all-to-all-start.2) | async-done | bytes 786464 | tf_op jit(solution)/shard_map/all_to_all | solution.py:175
  131.6 3.4 %slice_reduce_fusion.2 = (bf16[32,3072]{1,0:T(8,128)(2,1)S(1)}, bf16[32,3072]{1,0:T(8,128)(2,1)S(1)}, bf16[32,3072]{1,0:T(8,128)(2,1)S(1)}, bf16[32,3072]{1,0:T(8,128)(2,1)S(1)}) fusion(bf16[32,4,3072]{2,1,0:T(4,128)(2,1)S(1)} %reshape.284), kind=kLoop, calls=%fused_computation.71 | loop fusion | bytes 1572864 | tf_op jit(solution)/shard_map/slice | solution.py:108
  142.4 31.6 %all-reduce.7.cloned.1.call-done = (f32[512,512]{1,0:T(8,128)}, f32[512,512]{1,0:T(8,128)}) async-done(((f32[512,512]{1,0:T(8,128)}, f32[512,512]{1,0:T(8,128)}), (f32[512,512]{1,0:T(8,128)}, f32[512,512]{1,0:T(8,128)})) %all-reduce.7.cloned.1.call-update) | async-done | bytes 2097168 | tf_op jit(solution)/shard_map/psum | solution.py:181
  174.1 3.4 %collective-permute-start.2 = (f32[32,1280]{1,0:T(8,128)S(1)}, f32[32,1280]{1,0:T(8,128)S(1)}, u32[]{:S(2)}, u32[]{:S(2)}) collective-permute-start(f32[32,1280]{1,0:T(8,128)S(1)} %get-tuple-element.31), channel_id=1, source_target_pairs={{0,4},{4,8},{8,12},{12,16},{16,20},{20,24},{24,28},{1,5},{5,9},{9,... | collective-permute-start | bytes 491528 | tf_op jit(solution)/shard_map/ppermute | solution.py:19
  180.7 4.1 %collective-permute-done.3 = f32[32,1280]{1,0:T(8,128)S(1)} collective-permute-done((f32[32,1280]{1,0:T(8,128)S(1)}, f32[32,1280]{1,0:T(8,128)S(1)}, u32[]{:S(2)}, u32[]{:S(2)}) %collective-permute-start.3) | collective-permute-done | bytes 163872 | tf_op jit(solution)/shard_map/ppermute | solution.py:21
  185.8 7.2 %all-to-all-start.3 = ((f32[32,8,160]{2,0,1:T(8,128)}), f32[32,8,160]{2,0,1:T(8,128)S(1)}, u32[]{:S(2)}, u32[]{:S(2)}) async-start(f32[32,8,160]{2,0,1:T(8,128)} %copy.63), calls=%async_computation.3 | async-start | bytes 524288 | tf_op jit(solution)/shard_map/all_to_all | solution.py:189
  193.0 6.1 %psum.44 = f32[512]{0:T(512)S(1)} all-reduce(f32[512]{0:T(512)S(1)} %get-tuple-element.45), channel_id=1, replica_groups=mesh['band'=8,'rep'=4] {'rep'}, use_global_device_ids=true, to_apply=%region_11.12 | all-reduce | flops 512 | bytes 4096 | tf_op jit(solution)/shard_map/psum | solution.py:181
  199.1 22.9 %psum.45 = f32[512]{0:T(512)} all-reduce(f32[512]{0:T(512)S(1)} %psum.44), channel_id=1, replica_groups=mesh['band'=8,'rep'=4] {'band'}, use_global_device_ids=true, to_apply=%region_12.13 | all-reduce | flops 512 | bytes 4096 | tf_op jit(solution)/shard_map/psum | solution.py:181
  224.1 61.7 %all-reduce.5.cloned.1.call-done = (f32[512,512]{1,0:T(8,128)}, f32[512,512]{1,0:T(8,128)}) async-done(((f32[512,512]{1,0:T(8,128)}, f32[512,512]{1,0:T(8,128)}), (f32[512,512]{1,0:T(8,128)}, f32[512,512]{1,0:T(8,128)})) %all-reduce.5.cloned.1.call-update) | async-done | bytes 2097168 | tf_op jit(solution)/shard_map/psum | solution.py:181
  (135 shorter events, 66.2 us)
Async XLA Ops:
  7.2 103.8 %copy-start = (bf16[512,512]{1,0:T(8,128)(2,1)S(1)}, bf16[512,512]{1,0:T(8,128)(2,1)}, u32[]{:S(2)}) copy-start(bf16[512,512]{1,0:T(8,128)(2,1)} %param.12) | copy-start | bytes 1572868
  10.8 28.9 %copy-start.18 = (s32[512,1]{0,1:T(1,128)}, s32[512,1]{0,1:T(1,128)S(1)}, u32[]{:S(2)}) copy-start(s32[512,1]{0,1:T(1,128)S(1)} %compare_select_fusion) | copy-start | bytes 6148
  14.6 14.9 %all-to-all-start = ((bf16[35,8,160]{2,0,1:T(8,128)(2,1)}), bf16[35,8,160]{2,0,1:T(8,128)(2,1)S(1)}, u32[]{:S(2)}, u32[]{:S(2)}) async-start(bf16[35,8,160]{2,0,1:T(8,128)(2,1)} %copy.50), calls=%async_computation | async-start | bytes 327680 | tf_op jit(solution)/shard_map/all_to_all | solution.py:140
  29.7 6.1 %collective-permute-start = (bf16[35,1280]{1,0:T(8,128)(2,1)S(1)}, bf16[35,1280]{1,0:T(8,128)(2,1)S(1)}, u32[]{:S(2)}, u32[]{:S(2)}) collective-permute-start(bf16[35,1280]{1,0:T(8,128)(2,1)S(1)} %all_to_all.42), channel_id=1, source_target_pairs={{0,4},{4,8},{8,12},{12,16},{16,20},{20,24},{24,28},{1,5},{5,9},{9,... | collective-permute-start | bytes 268808 | tf_op jit(solution)/shard_map/ppermute | solution.py:19
  32.6 6.6 %collective-permute-start.1 = (bf16[35,1280]{1,0:T(8,128)(2,1)S(1)}, bf16[35,1280]{1,0:T(8,128)(2,1)S(1)}, u32[]{:S(2)}, u32[]{:S(2)}) collective-permute-start(bf16[35,1280]{1,0:T(8,128)(2,1)S(1)} %all_to_all.42), channel_id=1, source_target_pairs={{4,0},{8,4},{12,8},{16,12},{20,16},{24,20},{28,24},{5,1},{9,5},{13... | collective-permute-start | bytes 268808 | tf_op jit(solution)/shard_map/ppermute | solution.py:21
  44.2 11.1 %copy-start.1 = (bf16[4,256,3840]{2,1,0:T(8,128)(2,1)}, bf16[4,256,3840]{2,1,0:T(8,128)(2,1)S(1)}, u32[]{:S(2)}) copy-start(bf16[4,256,3840]{2,1,0:T(8,128)(2,1)S(1)} %exponential_convert_fusion) | copy-start | bytes 23592964
  87.0 4.7 %copy-start.15 = (f32[12,256]{1,0:T(8,128)S(1)}, f32[12,256]{1,0:T(8,128)}, u32[]{:S(2)}) copy-start(f32[12,256]{1,0:T(8,128)} %fusion.8) | copy-start | bytes 36868
  87.0 4.7 %copy-start.16 = (f32[12,256]{1,0:T(8,128)S(1)}, f32[12,256]{1,0:T(8,128)}, u32[]{:S(2)}) copy-start(f32[12,256]{1,0:T(8,128)} %fusion.12) | copy-start | bytes 36868
  87.0 4.8 %copy-start.17 = (f32[12,256]{1,0:T(8,128)S(1)}, f32[12,256]{1,0:T(8,128)}, u32[]{:S(2)}) copy-start(f32[12,256]{1,0:T(8,128)} %fusion.16) | copy-start | bytes 36868
  94.9 4.5 %copy-start.4 = (bf16[512,3,256]{2,0,1:T(8,128)(2,1)S(1)}, bf16[512,3,256]{2,0,1:T(8,128)(2,1)}, u32[]{:S(2)}) copy-start(bf16[512,3,256]{2,0,1:T(8,128)(2,1)} %param.15) | copy-start | bytes 2359300
  95.9 15.1 %all-to-all-start.1 = ((bf16[128,4,768]{2,0,1:T(8,128)(2,1)}), bf16[128,4,768]{2,0,1:T(8,128)(2,1)S(1)}, u32[]{:S(2)}, u32[]{:S(2)}) async-start(bf16[128,4,768]{2,0,1:T(8,128)(2,1)} %copy.56), calls=%async_computation.1 | async-start | bytes 1572864 | tf_op jit(solution)/shard_map/all_to_all | solution.py:147
  100.8 10.2 %copy-start.21 = (f32[512]{0:T(512)S(1)}, f32[512]{0:T(512)}, u32[]{:S(2)}) copy-start(f32[512]{0:T(512)} %param.13) | copy-start | bytes 6148
  102.6 9.1 %copy-start.5 = (bf16[512,3,256]{0,2,1:T(8,128)(2,1)S(1)}, bf16[512,3,256]{0,2,1:T(8,128)(2,1)}, u32[]{:S(2)}) copy-start(bf16[512,3,256]{0,2,1:T(8,128)(2,1)} %copy.48) | copy-start | bytes 2359300
  102.6 9.1 %copy-start.20 = (bf16[512,512]{1,0:T(8,128)(2,1)S(1)}, bf16[512,512]{1,0:T(8,128)(2,1)}, u32[]{:S(2)}) copy-start(bf16[512,512]{1,0:T(8,128)(2,1)} %param.14) | copy-start | bytes 1572868
  115.1 15.6 %all-to-all-start.2 = ((bf16[4,128,768]{2,1,0:T(8,128)(2,1)}), bf16[4,128,768]{2,1,0:T(8,128)(2,1)S(1)}, u32[]{:S(2)}, u32[]{:S(2)}) async-start(bf16[4,128,768]{2,1,0:T(8,128)(2,1)} %bitcast.158), calls=%async_computation.2 | async-start | bytes 1572864 | tf_op jit(solution)/shard_map/all_to_all | solution.py:175
  118.6 55.3 %all-reduce.7.cloned.1.call-start = ((), (), s32[]{:S(2)}) async-start(), calls=%async_computation.5 | async-start | bytes 4194304 | tf_op jit(solution)/shard_map/psum | solution.py:181
  123.4 162.4 %all-reduce.5.cloned.1.call-start = ((), (), s32[]{:S(2)}) async-start(), calls=%async_computation.4 | async-start | bytes 4194304 | tf_op jit(solution)/shard_map/psum | solution.py:181
  131.3 3.7 %copy-start.14 = (f32[12,3840]{1,0:T(8,128)S(1)}, f32[12,3840]{1,0:T(8,128)}, u32[]{:S(2)}) copy-start(f32[12,3840]{1,0:T(8,128)} %get-tuple-element.33) | copy-start | bytes 552964
  131.6 8.8 %slice-start = ((s8[7864320]{0:T(1024)(128)(4,1)}), s8[3670016]{0:T(1024)(128)(4,1)S(1)}, s32[]{:S(2)}) async-start(s8[7864320]{0:T(1024)(128)(4,1)} %bitcast.149), calls=%async_computation.6 | async-start | bytes 7340032
  135.0 5.4 %slice-start.1 = ((s8[7864320]{0:T(1024)(128)(4,1)}), s8[4194304]{0:T(1024)(128)(4,1)S(1)}, s32[]{:S(2)}) async-start(s8[7864320]{0:T(1024)(128)(4,1)} %bitcast.149), calls=%async_computation.7 | async-start | bytes 8388608
  174.1 18.9 %copy-start.19 = (s32[512,1]{0,1:T(1,128)S(1)}, s32[512,1]{0,1:T(1,128)}, u32[]{:S(2)}) copy-start(s32[512,1]{0,1:T(1,128)} %copy-done.18) | copy-start | bytes 6148
  174.1 6.6 %collective-permute-start.2 = (f32[32,1280]{1,0:T(8,128)S(1)}, f32[32,1280]{1,0:T(8,128)S(1)}, u32[]{:S(2)}, u32[]{:S(2)}) collective-permute-start(f32[32,1280]{1,0:T(8,128)S(1)} %get-tuple-element.31), channel_id=1, source_target_pairs={{0,4},{4,8},{8,12},{12,16},{16,20},{20,24},{24,28},{1,5},{5,9},{9,... | collective-permute-start | bytes 491528 | tf_op jit(solution)/shard_map/ppermute | solution.py:19
  177.5 7.3 %collective-permute-start.3 = (f32[32,1280]{1,0:T(8,128)S(1)}, f32[32,1280]{1,0:T(8,128)S(1)}, u32[]{:S(2)}, u32[]{:S(2)}) collective-permute-start(f32[32,1280]{1,0:T(8,128)S(1)} %get-tuple-element.32), channel_id=1, source_target_pairs={{4,0},{8,4},{12,8},{16,12},{20,16},{24,20},{28,24},{5,1},{9,5},{13... | collective-permute-start | bytes 491528 | tf_op jit(solution)/shard_map/ppermute | solution.py:21
  185.8 36.2 %all-to-all-start.3 = ((f32[32,8,160]{2,0,1:T(8,128)}), f32[32,8,160]{2,0,1:T(8,128)S(1)}, u32[]{:S(2)}, u32[]{:S(2)}) async-start(f32[32,8,160]{2,0,1:T(8,128)} %copy.63), calls=%async_computation.3 | async-start | bytes 524288 | tf_op jit(solution)/shard_map/all_to_all | solution.py:189
  (12 other events, 27.1 us)
Sparse Core Ops, SparseCore 0:
  123.5 50.4 all-reduce.6
  177.6 108.0 all-reduce.4
